TPU v7x, 32 devices: a whole 2x2x4 slice. The times are simulated.
32 devices in a mesh: pipe: 4 (over z), tensor: 4 (over x, core), dp: 2 (over y).
Axes of the slice: x: 2, y: 2, z: 4, core: 2. Of those that a mesh axis runs over, the one named last changes fastest.
Arguments:
- inputs: bfloat16 [2, 128, 4096], P(None, ('tensor', 'dp')), may hold values from -6 to 6
- weights: bfloat16 [2, 4, 4096, 4096], P(None, 'pipe', None, 'tensor'), may hold values from -0.09375 to 0.09375
- norm_gains: float32 [2, 4, 4096], P(None, 'pipe'), may hold values from 0.1 to 1.9
- cotangent: bfloat16 [2, 128, 4096], P(None, ('tensor', 'dp')), may hold values from -6 to 6
Outputs:
- act_factor: bfloat16 [4096, 2, 4, 4096], P(('tensor', 'dp'), None, 'pipe')
- grad_factor: bfloat16 [4096, 2, 4, 4096], P(('tensor', 'dp'), None, 'pipe')
All inputs are finite; a program needn't handle non-finite values.
Results may differ from a plain program's by a relative error of at most 0.025.
Values may be sent and summed in bfloat16 or wider, within the bound.
A program may use at most 192 MiB of HBM per device.

v0:
```python
import jax
import jax.numpy as jnp
from jax import lax
from jax.sharding import PartitionSpec as P

EPSILON = 1e-05


def passed_along(array, axis, by):
    peers = lax.axis_size(axis)
    return lax.ppermute(array, axis, [(i, (i + by) % peers) for i in range(peers)])


def normalize(hidden, gain_row):
    hidden_wide = hidden.astype(jnp.float32)
    inverse_rms = lax.rsqrt(jnp.mean(hidden_wide * hidden_wide, axis=-1, keepdims=True) + EPSILON)
    normed = (hidden_wide * inverse_rms * gain_row).astype(jnp.bfloat16)
    return (hidden_wide, inverse_rms, normed)


def rounded(values):
    return lax.optimization_barrier(values.astype(jnp.bfloat16)).astype(jnp.float32)


def body(inputs, weights, norm_gains, cotangent):
    micro_count, shard_rows, features = inputs.shape
    slot_count = weights.shape[0]
    quarter = weights.shape[3]
    tensor_count = lax.axis_size("tensor")
    pipe_count = lax.axis_size("pipe")
    dp_count = lax.axis_size("dp")
    layer_count = slot_count * pipe_count
    section_index = lax.axis_index("pipe")
    column = lax.axis_index("tensor")
    tick_count = micro_count + layer_count - 1
    group_rows = tensor_count * shard_rows
    group_size = micro_count * group_rows
    stash_count = slot_count * micro_count + 1
    own_rows = quarter // dp_count
    inv_tokens = 1.0 / (micro_count * group_rows * dp_count)
    row_base = column * quarter
    normed_stash = jnp.zeros((stash_count, group_rows, features), jnp.bfloat16)
    hidden_stash = jnp.zeros((stash_count, shard_rows, features), jnp.bfloat16)
    grad_stash = jnp.zeros((stash_count, group_rows, features), jnp.bfloat16)
    received = jnp.zeros((shard_rows, features), jnp.bfloat16)
    for moment in range(tick_count):
        micro_index = (moment - section_index) % pipe_count
        layer_index = moment - micro_index
        usable = (micro_index < micro_count) & (layer_index >= 0) & (layer_index < layer_count)
        slot_index = jnp.clip(layer_index // pipe_count, 0, slot_count - 1)
        target = jnp.where(usable, slot_index * micro_count + micro_index, stash_count - 1)
        if moment < micro_count:
            current = jnp.where(section_index == 0, inputs[moment], received)
        else:
            current = received
        weight = lax.dynamic_index_in_dim(weights, slot_index, 0, keepdims=False)[0]
        gain_row = lax.dynamic_index_in_dim(norm_gains, slot_index, 0, keepdims=False)[0]
        hidden_wide, inverse_rms, normed = normalize(current, gain_row)
        gathered = lax.all_gather(normed, "tensor", axis=0, tiled=True)
        normed_stash = lax.dynamic_update_index_in_dim(normed_stash, gathered, target, 0)
        hidden_stash = lax.dynamic_update_index_in_dim(hidden_stash, current, target, 0)
        if moment + 1 < tick_count:
            active = usable & (layer_index + 1 < layer_count)
            product = lax.cond(
                active,
                lambda: jnp.dot(gathered, weight, preferred_element_type=jnp.float32).astype(
                    jnp.bfloat16
                ),
                lambda: jnp.zeros((group_rows, quarter), jnp.bfloat16),
            )
            returned = lax.all_to_all(product, "tensor", split_axis=0, concat_axis=1, tiled=True)
            following = (hidden_wide + returned.astype(jnp.float32)).astype(jnp.bfloat16)
            received = passed_along(following, "pipe", 1)
    act_tokens = normed_stash[: stash_count - 1].reshape(slot_count, group_size, features)
    received = jnp.zeros((shard_rows, features), jnp.bfloat16)
    for moment in range(tick_count):
        micro_index = (section_index + 1 - layer_count + moment) % pipe_count
        depth = moment - micro_index
        layer_index = layer_count - 1 - depth
        usable = (micro_index < micro_count) & (depth >= 0) & (depth < layer_count)
        slot_index = jnp.clip(layer_index // pipe_count, 0, slot_count - 1)
        target = jnp.where(usable, slot_index * micro_count + micro_index, stash_count - 1)
        if moment < micro_count:
            current = jnp.where(section_index == pipe_count - 1, cotangent[moment], received)
        else:
            current = received
        gathered = lax.all_gather(current, "tensor", axis=0, tiled=True)
        grad_stash = lax.dynamic_update_index_in_dim(grad_stash, gathered, target, 0)
        if moment + 1 < tick_count:
            active = usable & (layer_index > 0)
            weight = lax.dynamic_index_in_dim(weights, slot_index, 0, keepdims=False)[0]
            gain_row = lax.dynamic_index_in_dim(norm_gains, slot_index, 0, keepdims=False)[0]
            own_columns = lax.dynamic_slice_in_dim(gathered, row_base, quarter, 1)

            def partial_rows(
                row_start, row_total, own_columns=own_columns, weight=weight, active=active
            ):
                piece = own_columns
                return lax.cond(
                    active,
                    lambda: lax.dot_general(
                        piece, weight, (((1,), (1,)), ((), ())), preferred_element_type=jnp.float32
                    ),
                    lambda: jnp.zeros((row_total, features), jnp.float32),
                )

            back_sum = lax.psum_scatter(
                partial_rows(jnp.int32(0), shard_rows * lax.axis_size("tensor")).astype(
                    jnp.bfloat16
                ),
                "tensor",
                scatter_dimension=0,
                tiled=True,
            ).astype(jnp.float32)
            stored = lax.dynamic_index_in_dim(hidden_stash, target, 0, keepdims=False)
            hidden_wide = stored.astype(jnp.float32)
            inverse_rms = lax.rsqrt(
                jnp.mean(hidden_wide * hidden_wide, axis=-1, keepdims=True) + EPSILON
            )
            scaled = gain_row * back_sum
            inner = jnp.mean(hidden_wide * scaled, axis=-1, keepdims=True)
            following = (
                current.astype(jnp.float32)
                + inverse_rms * scaled
                - inverse_rms**3 * hidden_wide * inner
            ).astype(jnp.bfloat16)
            received = passed_along(following, "pipe", -1)
    grad_tokens = grad_stash[: stash_count - 1].reshape(slot_count, group_size, features)
    own_base = (column * dp_count + lax.axis_index("dp")) * own_rows
    empty = jnp.zeros((own_rows, slot_count, 1, features), jnp.float32)
    pieces = (
        lax.all_gather(act_tokens, "dp", axis=1, tiled=True),
        lax.all_gather(grad_tokens, "dp", axis=1, tiled=True),
    )

    def one_group(group_pick, totals):
        updated = []
        for factor_pick in range(2):
            tokens_block = lax.dynamic_slice_in_dim(
                pieces[factor_pick], group_pick * group_size, group_size, 1
            )
            partials = []
            for slot_pick in range(slot_count):
                tokens_one = tokens_block[slot_pick]
                columns = lax.dynamic_slice_in_dim(tokens_one, own_base, own_rows, 1)
                gram = lax.dot_general(
                    columns,
                    tokens_one,
                    (((0,), (0,)), ((), ())),
                    preferred_element_type=jnp.float32,
                )
                partials.append(rounded(gram * inv_tokens))
            updated.append(totals[factor_pick] + jnp.stack(partials, 1)[:, :, None, :])
        return (updated[0], updated[1])

    act_total, grad_total = lax.fori_loop(
        0, pieces[0].shape[1] // group_size, one_group, (empty, empty)
    )
    act_factor = act_total.astype(jnp.bfloat16)
    grad_factor = grad_total.astype(jnp.bfloat16)
    return (act_factor, grad_factor)


def solution(mesh):
    in_specs = (
        P(None, ("tensor", "dp"), None),
        P(None, "pipe", None, "tensor"),
        P(None, "pipe", None),
        P(None, ("tensor", "dp"), None),
    )
    out_specs = (P(("tensor", "dp"), None, "pipe", None), P(("tensor", "dp"), None, "pipe", None))
    return jax.shard_map(body, mesh=mesh, in_specs=in_specs, out_specs=out_specs, check_vma=False)
```

profile of v0, /device:TPU:0, one launch (start us, length us, event | category | flops | bytes accessed | tf_op | source)
XLA Modules:
  0.0 747.0 jit_solution(15114251936575644437)
XLA Ops:
  12.7 8.6 %all_gather.60 = bf16[64,4096]{1,0:T(8,128)(2,1)S(1)} all-gather(bf16[16,4096]{1,0:T(8,128)(2,1)S(1)} %fusion.157), channel_id=1, replica_groups=mesh['pipe'=4,'tensor'=4,'dp'=2] {'tensor'}, dimensions={0}, use_global_device_ids=true | all-gather | bytes 655360 | tf_op jit(solution)/shard_map/all_gather | solution.py:59
  21.4 5.6 conditional.16
  21.4 5.6 fusion.6
  30.4 4.5 all-to-all-done
  35.2 6.6 collective-permute-done
  42.1 7.0 all_gather.61
  49.1 5.1 conditional.17
  49.1 5.1 fusion.16
  54.2 7.0 all_to_all.104
  61.4 6.7 collective-permute-done.1
  68.4 7.0 all_gather.62
  75.4 7.0 all_to_all.105
  82.4 3.6 collective-permute-start.2
  89.5 7.0 all_gather.63
  96.5 7.1 all_to_all.106
  105.5 6.1 collective-permute-done.3
  111.9 7.0 all_gather.64
  118.8 5.8 conditional.20
  118.8 5.8 fusion.46
  128.0 4.5 all-to-all-done.4
  132.7 7.0 all-gather
  141.3 7.7 %all_gather.65 = bf16[64,4096]{1,0:T(8,128)(2,1)} all-gather(bf16[16,4096]{1,0:T(8,128)(2,1)S(1)} %fusion.145), channel_id=1, replica_groups=mesh['pipe'=4,'tensor'=4,'dp'=2] {'tensor'}, dimensions={0}, use_global_device_ids=true | all-gather | bytes 655360 | tf_op jit(solution)/shard_map/all_gather | solution.py:59
  149.0 5.8 conditional.21
  149.0 5.8 fusion.56
  158.2 4.5 all-to-all-done.5
  162.9 7.9 %collective-permute-done.5 = bf16[16,4096]{1,0:T(8,128)(2,1)S(1)} collective-permute-done((bf16[16,4096]{1,0:T(8,128)(2,1)S(1)}, bf16[16,4096]{1,0:T(8,128)(2,1)S(1)}, u32[]{:S(2)}, u32[]{:S(2)}) %collective-permute-start.5) | collective-permute-done | bytes 131104 | tf_op jit(solution)/shard_map/ppermute | solution.py:11
  171.0 7.0 all_gather.66
  182.0 4.5 all-to-all-done.6
  189.1 4.4 collective-permute-done.6
  193.7 7.0 all_gather.67
  204.7 4.5 all-to-all-done.7
  210.8 5.4 collective-permute-done.7
  219.2 6.3 collective-permute-start.8
  228.0 7.0 all_gather.71
  238.5 26.8 %reduce-scatter.11.cloned.1.call-done = bf16[16,4096]{1,0:T(8,128)(2,1)} async-done(((bf16[64,4096]{1,0:T(8,128)(2,1)}), bf16[16,4096]{1,0:T(8,128)(2,1)}) %reduce-scatter.11.cloned.1.call-update) | async-done | bytes 131088 | tf_op jit(solution)/shard_map/reduce_scatter | solution.py:107
  274.4 7.3 all_gather.72
  285.7 23.5 %reduce-scatter.13.cloned.1.call-done = bf16[16,4096]{1,0:T(8,128)(2,1)} async-done(((bf16[64,4096]{1,0:T(8,128)(2,1)}), bf16[16,4096]{1,0:T(8,128)(2,1)}) %reduce-scatter.13.cloned.1.call-update) | async-done | bytes 131088 | tf_op jit(solution)/shard_map/reduce_scatter | solution.py:107
  311.4 3.4 collective-permute-start.10
  317.3 6.9 all_gather.73
  324.3 6.9 conditional.27
  324.3 6.9 fusion.95
  334.4 16.6 %reduce-scatter.15.cloned.1.call-done = bf16[16,4096]{1,0:T(8,128)(2,1)} async-done(((bf16[64,4096]{1,0:T(8,128)(2,1)}), bf16[16,4096]{1,0:T(8,128)(2,1)}) %reduce-scatter.15.cloned.1.call-update) | async-done | bytes 131088 | tf_op jit(solution)/shard_map/reduce_scatter | solution.py:107
  359.1 6.9 all_gather.74
  366.0 6.9 conditional.28
  366.0 6.9 fusion.100
  376.1 20.3 %reduce-scatter.17.cloned.1.call-done = bf16[16,4096]{1,0:T(8,128)(2,1)} async-done(((bf16[64,4096]{1,0:T(8,128)(2,1)}), bf16[16,4096]{1,0:T(8,128)(2,1)}) %reduce-scatter.17.cloned.1.call-update) | async-done | bytes 131088 | tf_op jit(solution)/shard_map/reduce_scatter | solution.py:107
  404.5 6.9 all_gather.75
  415.5 26.3 %reduce-scatter.19.cloned.1.call-done = bf16[16,4096]{1,0:T(8,128)(2,1)} async-done(((bf16[64,4096]{1,0:T(8,128)(2,1)}), bf16[16,4096]{1,0:T(8,128)(2,1)}) %reduce-scatter.19.cloned.1.call-update) | async-done | bytes 131088 | tf_op jit(solution)/shard_map/reduce_scatter | solution.py:107
  443.9 3.4 collective-permute-start.13
  450.5 6.9 all_gather.76
  459.3 25.9 %reduce-scatter.21.cloned.1.call-done = bf16[16,4096]{1,0:T(8,128)(2,1)} async-done(((bf16[64,4096]{1,0:T(8,128)(2,1)}), bf16[16,4096]{1,0:T(8,128)(2,1)}) %reduce-scatter.21.cloned.1.call-update) | async-done | bytes 131088 | tf_op jit(solution)/shard_map/reduce_scatter | solution.py:107
  490.8 6.9 all_gather.68
  497.8 7.7 %all_gather.77 = bf16[64,4096]{1,0:T(8,128)(2,1)} all-gather(bf16[16,4096]{1,0:T(8,128)(2,1)S(1)} %collective-permute-done.14), channel_id=1, replica_groups=mesh['pipe'=4,'tensor'=4,'dp'=2] {'tensor'}, dimensions={0}, use_global_device_ids=true | all-gather | bytes 655360 | tf_op jit(solution)/shard_map/all_gather | solution.py:87
  519.3 11.0 %reduce-scatter.23.cloned.1.call-done = bf16[16,4096]{1,0:T(8,128)(2,1)} async-done(((bf16[64,4096]{1,0:T(8,128)(2,1)}), bf16[16,4096]{1,0:T(8,128)(2,1)}) %reduce-scatter.23.cloned.1.call-update) | async-done | bytes 131088 | tf_op jit(solution)/shard_map/reduce_scatter | solution.py:107
  538.4 6.5 all_gather.78
  546.4 25.0 %all-gather.4.cloned.1.call-done = bf16[2,256,4096]{2,1,0:T(8,128)(2,1)} async-done(((bf16[2,128,4096]{2,1,0:T(8,128)(2,1)}), bf16[2,256,4096]{2,1,0:T(8,128)(2,1)}) %all-gather.4.cloned.1.call-update) | async-done | bytes 4194320 | tf_op jit(solution)/shard_map/all_gather | solution.py:132
  571.5 58.6 %all-gather.6.cloned.1.call-done = bf16[2,256,4096]{2,1,0:T(8,128)(2,1)} async-done(((bf16[2,128,4096]{2,1,0:T(8,128)(2,1)}), bf16[2,256,4096]{2,1,0:T(8,128)(2,1)}) %all-gather.6.cloned.1.call-update) | async-done | bytes 4194320 | tf_op jit(solution)/shard_map/all_gather | solution.py:133
  630.1 62.1 %while.18 = (s32[]{:T(128)}, f32[512,2,1,4096]{3,0,1,2:T(8,128)}, f32[512,2,1,4096]{3,0,1,2:T(8,128)}, bf16[2,256,4096]{2,1,0:T(8,128)(2,1)}, s32[]{:T(128)}, /*...) while((s32[]{:T(128)}, f32[512,2,1,4096]{3,0,1,2:T(8,128)}, ...), condition=%wide.region_66.67_spmd.clone, body=%wide.region_65.66_spmd.clone.sunk | while | flops 2197815296 | bytes 105390264 | solution.py:156
  632.7 4.6 multiply_convert_fusion.10
  642.5 14.2 %convert_add_fusion.12 = (f32[512,2,1,4096]{3,0,1,2:T(8,128)}, f32[512,2,1,4096]{3,0,1,2:T(8,128)}) fusion(f32[512,2,1,4096]{3,0,1,2:T(8,128)} %get-tuple-element.770, bf16[512,1,4096]{2,0,1:T(8,128)(2,1)S(1)} %bitcast.333, bf16[512,1,4096]{2,0,1:T(8,128)(2,1)S(1)} %bitcast.331, pred[]{:T(512)S(6)} %compare.57, bf16[512,1,4096]{2,0,1:T(8,128)(2,1)} %bitcast.334, ...), kind=kLoop, calls=%fused_computation.88.clone.1 | loop fusion | flops 33554432 | bytes 83886080 | tf_op jit(solution)/shard_map/while/body/eval_jaxpr/add | solution.py:153
  659.2 4.6 multiply_convert_fusion.10
  669.1 23.1 %convert_add_fusion.12 = (f32[512,2,1,4096]{3,0,1,2:T(8,128)}, f32[512,2,1,4096]{3,0,1,2:T(8,128)}) fusion(f32[512,2,1,4096]{3,0,1,2:T(8,128)} %get-tuple-element.770, bf16[512,1,4096]{2,0,1:T(8,128)(2,1)S(1)} %bitcast.333, bf16[512,1,4096]{2,0,1:T(8,128)(2,1)S(1)} %bitcast.331, pred[]{:T(512)S(6)} %compare.57, bf16[512,1,4096]{2,0,1:T(8,128)(2,1)} %bitcast.334, ...), kind=kLoop, calls=%fused_computation.88.clone.1 | loop fusion | flops 33554432 | bytes 83886080 | tf_op jit(solution)/shard_map/while/body/eval_jaxpr/add | solution.py:153
  692.2 28.6 %copy.38 = bf16[512,2,1,4096]{3,1,2,0:T(2,128)(2,1)} copy(f32[512,2,1,4096]{3,0,1,2:T(8,128)} %get-tuple-element.635) | data formatting | bytes 25165824 | tf_op jit(solution)/shard_map/while | solution.py:156
  720.7 18.6 %copy.39 = bf16[512,2,1,4096]{3,1,2,0:T(2,128)(2,1)} copy(f32[512,2,1,4096]{3,0,1,2:T(8,128)S(1)} %copy-done) | data formatting | bytes 25165824 | tf_op jit(solution)/shard_map/while | solution.py:156
  (205 shorter events, 144.5 us)
Async XLA Ops:
  8.0 27.0 %copy-start.3 = (bf16[2,16,4096]{2,1,0:T(8,128)(2,1)S(1)}, bf16[2,16,4096]{2,1,0:T(8,128)(2,1)}, u32[]{:S(2)}) copy-start(bf16[2,16,4096]{2,1,0:T(8,128)(2,1)} %param.38) | copy-start | bytes 786436
  27.0 7.9 %all-to-all-start = ((bf16[4,16,1024]{2,1,0:T(8,128)(2,1)}), bf16[4,16,1024]{2,1,0:T(8,128)(2,1)S(1)}, u32[]{:S(2)}, u32[]{:S(2)}) async-start(bf16[4,16,1024]{2,1,0:T(8,128)(2,1)} %bitcast.29), calls=%async_computation | async-start | bytes 262144 | tf_op jit(solution)/shard_map/all_to_all | solution.py:71
  35.0 6.8 collective-permute-start
  61.3 6.8 collective-permute-start.1
  82.4 6.8 collective-permute-start.2
  96.5 31.5 %copy-start.4 = (bf16[2,16,4096]{2,1,0:T(8,128)(2,1)S(1)}, bf16[2,16,4096]{2,1,0:T(8,128)(2,1)}, u32[]{:S(2)}) copy-start(bf16[2,16,4096]{2,1,0:T(8,128)(2,1)} %param.41) | copy-start | bytes 786436
  103.7 7.9 %collective-permute-start.3 = (bf16[16,4096]{1,0:T(8,128)(2,1)S(1)}, bf16[16,4096]{1,0:T(8,128)(2,1)S(1)}, u32[]{:S(2)}, u32[]{:S(2)}) collective-permute-start(bf16[16,4096]{1,0:T(8,128)(2,1)S(1)} %fusion.138), channel_id=1, source_target_pairs={{0,8},{8,16},{16,24},{24,0},{1,9},{9,17},{17,25},{25,1},{2,10},{10... | collective-permute-start | bytes 393224 | tf_op jit(solution)/shard_map/ppermute | solution.py:11
  124.6 7.9 %all-to-all-start.4 = ((bf16[4,16,1024]{2,1,0:T(8,128)(2,1)}), bf16[4,16,1024]{2,1,0:T(8,128)(2,1)S(1)}, u32[]{:S(2)}, u32[]{:S(2)}) async-start(bf16[4,16,1024]{2,1,0:T(8,128)(2,1)} %bitcast.45), calls=%async_computation.4 | async-start | bytes 262144 | tf_op jit(solution)/shard_map/all_to_all | solution.py:71
  127.9 88.2 %reduce-scatter.9.cloned.1.call-start = ((), (), s32[]{:S(2)}) async-start(), calls=%async_computation.17 | async-start | bytes 655360 | tf_op jit(solution)/shard_map/reduce_scatter | solution.py:107
  132.6 8.4 %collective-permute-start.4 = (bf16[16,4096]{1,0:T(8,128)(2,1)S(1)}, bf16[16,4096]{1,0:T(8,128)(2,1)S(1)}, u32[]{:S(2)}, u32[]{:S(2)}) collective-permute-start(bf16[16,4096]{1,0:T(8,128)(2,1)S(1)} %fusion.142), channel_id=1, source_target_pairs={{0,8},{8,16},{16,24},{24,0},{1,9},{9,17},{17,25},{25,1},{2,10},{10... | collective-permute-start | bytes 393224 | tf_op jit(solution)/shard_map/ppermute | solution.py:11
  139.8 0.8 copy-start.1
  154.8 7.9 %all-to-all-start.5 = ((bf16[4,16,1024]{2,1,0:T(8,128)(2,1)}), bf16[4,16,1024]{2,1,0:T(8,128)(2,1)S(1)}, u32[]{:S(2)}, u32[]{:S(2)}) async-start(bf16[4,16,1024]{2,1,0:T(8,128)(2,1)} %bitcast.49), calls=%async_computation.5 | async-start | bytes 262144 | tf_op jit(solution)/shard_map/all_to_all | solution.py:71
  162.8 7.9 %collective-permute-start.5 = (bf16[16,4096]{1,0:T(8,128)(2,1)S(1)}, bf16[16,4096]{1,0:T(8,128)(2,1)S(1)}, u32[]{:S(2)}, u32[]{:S(2)}) collective-permute-start(bf16[16,4096]{1,0:T(8,128)(2,1)S(1)} %fusion.146), channel_id=1, source_target_pairs={{0,8},{8,16},{16,24},{24,0},{1,9},{9,17},{17,25},{25,1},{2,10},{10... | collective-permute-start | bytes 393224 | tf_op jit(solution)/shard_map/ppermute | solution.py:11
  178.6 7.9 %all-to-all-start.6 = ((bf16[4,16,1024]{2,1,0:T(8,128)(2,1)}), bf16[4,16,1024]{2,1,0:T(8,128)(2,1)S(1)}, u32[]{:S(2)}, u32[]{:S(2)}) async-start(bf16[4,16,1024]{2,1,0:T(8,128)(2,1)} %bitcast.53), calls=%async_computation.6 | async-start | bytes 262144 | tf_op jit(solution)/shard_map/all_to_all | solution.py:71
  186.6 6.8 collective-permute-start.6
  201.3 7.9 %all-to-all-start.7 = ((bf16[4,16,1024]{2,1,0:T(8,128)(2,1)}), bf16[4,16,1024]{2,1,0:T(8,128)(2,1)S(1)}, u32[]{:S(2)}, u32[]{:S(2)}) async-start(bf16[4,16,1024]{2,1,0:T(8,128)(2,1)} %bitcast.57), calls=%async_computation.7 | async-start | bytes 262144 | tf_op jit(solution)/shard_map/all_to_all | solution.py:71
  204.7 60.7 %reduce-scatter.11.cloned.1.call-start = ((), (), s32[]{:S(2)}) async-start(), calls=%async_computation.18 | async-start | bytes 655360 | tf_op jit(solution)/shard_map/reduce_scatter | solution.py:107
  209.3 6.8 collective-permute-start.7
  219.2 8.8 %collective-permute-start.8 = (bf16[16,4096]{1,0:T(8,128)(2,1)S(1)}, bf16[16,4096]{1,0:T(8,128)(2,1)S(1)}, u32[]{:S(2)}, u32[]{:S(2)}) collective-permute-start(bf16[16,4096]{1,0:T(8,128)(2,1)S(1)} %fusion.162), channel_id=1, source_target_pairs={{0,24},{8,0},{16,8},{24,16},{1,25},{9,1},{17,9},{25,17},{2,26},{10... | collective-permute-start | bytes 393224 | tf_op jit(solution)/shard_map/ppermute | solution.py:11
  235.0 0.8 copy-start.2
  235.9 73.4 %reduce-scatter.13.cloned.1.call-start = ((), (), s32[]{:S(2)}) async-start(), calls=%async_computation.19 | async-start | bytes 655360 | tf_op jit(solution)/shard_map/reduce_scatter | solution.py:107
  268.1 6.3 collective-permute-start.9
  282.6 68.5 %reduce-scatter.15.cloned.1.call-start = ((), (), s32[]{:S(2)}) async-start(), calls=%async_computation.20 | async-start | bytes 655360 | tf_op jit(solution)/shard_map/reduce_scatter | solution.py:107
  311.4 6.0 collective-permute-start.10
  331.2 65.1 %reduce-scatter.17.cloned.1.call-start = ((), (), s32[]{:S(2)}) async-start(), calls=%async_computation.21 | async-start | bytes 655360 | tf_op jit(solution)/shard_map/reduce_scatter | solution.py:107
  353.1 6.0 collective-permute-start.11
  373.0 68.7 %reduce-scatter.19.cloned.1.call-start = ((), (), s32[]{:S(2)}) async-start(), calls=%async_computation.22 | async-start | bytes 655360 | tf_op jit(solution)/shard_map/reduce_scatter | solution.py:107
  398.5 6.0 collective-permute-start.12
  412.3 73.0 %reduce-scatter.21.cloned.1.call-start = ((), (), s32[]{:S(2)}) async-start(), calls=%async_computation.23 | async-start | bytes 655360 | tf_op jit(solution)/shard_map/reduce_scatter | solution.py:107
  443.9 6.0 collective-permute-start.13
  449.9 0.6 copy-start.5
  458.5 71.8 %reduce-scatter.23.cloned.1.call-start = ((), (), s32[]{:S(2)}) async-start(), calls=%async_computation.24 | async-start | bytes 655360 | tf_op jit(solution)/shard_map/reduce_scatter | solution.py:107
  487.5 10.3 %collective-permute-start.14 = (bf16[16,4096]{1,0:T(8,128)(2,1)S(1)}, bf16[16,4096]{1,0:T(8,128)(2,1)S(1)}, u32[]{:S(2)}, u32[]{:S(2)}) collective-permute-start(bf16[16,4096]{1,0:T(8,128)(2,1)S(1)} %fusion.192), channel_id=1, source_target_pairs={{0,24},{8,0},{16,8},{24,16},{1,25},{9,1},{17,9},{25,17},{2,26},{10... | collective-permute-start | bytes 393224 | tf_op jit(solution)/shard_map/ppermute | solution.py:11
  506.4 65.1 %all-gather.4.cloned.1.call-start = ((), (), s32[]{:S(2)}) async-start(), calls=%async_computation.16 | async-start | bytes 6291456 | tf_op jit(solution)/shard_map/all_gather | solution.py:132
  512.7 117.4 %all-gather.6.cloned.1.call-start = ((), (), s32[]{:S(2)}) async-start(), calls=%async_computation.25 | async-start | bytes 6291456 | tf_op jit(solution)/shard_map/all_gather | solution.py:133
  532.4 6.0 collective-permute-start.15
  692.2 28.6 %copy-start = (f32[512,2,1,4096]{3,0,1,2:T(8,128)S(1)}, f32[512,2,1,4096]{3,0,1,2:T(8,128)}, u32[]{:S(2)}) copy-start(f32[512,2,1,4096]{3,0,1,2:T(8,128)} %get-tuple-element.634) | copy-start | bytes 50331652
Sparse Core Ops, SparseCore 0:
  140.8 28.8 reduce-scatter.8
  236.0 29.3 reduce-scatter.10
  282.7 26.5 reduce-scatter.12
  331.4 19.5 reduce-scatter.14
  373.1 23.2 reduce-scatter.16
  412.4 29.3 reduce-scatter.18
  458.6 26.6 reduce-scatter.20
  506.5 23.7 reduce-scatter.22
Sparse Core Ops, SparseCore 1:
  512.7 58.7 all-gather.3
  573.5 56.6 all-gather.5
where the time goes:
time: 757 us; the launch traced here: 747 us
  waiting for transfers between devices  306 us (40%)
  blocking collectives  149 us (20%)
  local copies, waits for them, and re-layouts  87.8 us (12%)
  other arithmetic  68.5 us (9%)
  matrix products  61 us (8%)
  starting transfers between devices  56.4 us (7%)
  between operations  17.6 us (2%)
    reduce_scatter x8, waiting for transfers between devices, body(): lax.psum_scatter(partial_rows(jnp.int32(0), shard_rows * lax.axis_size('t...  151 us
    all_gather x9, blocking collectives, body(): gathered = lax.all_gather(normed, 'tensor', axis=0, tiled=True)  65 us
    all_gather x9, blocking collectives, body(): gathered = lax.all_gather(current, 'tensor', axis=0, tiled=True)  63.2 us
    all_gather x1, waiting for transfers between devices, body(): lax.all_gather(grad_tokens, 'dp', axis=1, tiled=True)  58.6 us
    ppermute x16, waiting for transfers between devices, passed_along(): lax.ppermute(array, axis, [(i, (i + by) % peers) for i in range(peers)])  49.2 us
    while x2, local copies, waits for them, and re-layouts, body(): lax.fori_loop(0, pieces[0].shape[1] // group_size, one_group, (empty, emp...  47.2 us
    ppermute x16, starting transfers between devices, passed_along(): lax.ppermute(array, axis, [(i, (i + by) % peers) for i in range(peers)])  39.4 us
    add x2, other arithmetic, one_group(): updated.append(totals[factor_pick] + jnp.stack(partials, 1)[:, :, None, :])  37.3 us
  transfers between devices with their start and end apart: 31, of which 28 were waited for; matrix products, arithmetic and copies ran while one was open for 7% of the time, Pallas kernels for 0%

commit v1 on v0

--- a/solution.py
+++ b/solution.py
@@ -4,6 +4,12 @@
 from jax.sharding import PartitionSpec as P
 
 EPSILON = 1e-05
+
+
+def all_parts(block, name, dim):
+    parts = lax.all_gather(block, name, axis=0, tiled=False)
+    result = jnp.concatenate(parts, axis=dim)
+    return result
 
 
 def passed_along(array, axis, by):
@@ -128,10 +134,7 @@
     grad_tokens = grad_stash[: stash_count - 1].reshape(slot_count, group_size, features)
     own_base = (column * dp_count + lax.axis_index("dp")) * own_rows
     empty = jnp.zeros((own_rows, slot_count, 1, features), jnp.float32)
-    pieces = (
-        lax.all_gather(act_tokens, "dp", axis=1, tiled=True),
-        lax.all_gather(grad_tokens, "dp", axis=1, tiled=True),
-    )
+    pieces = (lax.all_gather(act_tokens, "dp", axis=1, tiled=True), all_parts(grad_tokens, "dp", 1))
 
     def one_group(group_pick, totals):
         updated = []

time: 757 us -> 757 us (level)
  no operation moved by 1% of the time
where the time goes in v1:
time: 757 us; the launch traced here: 747 us
  waiting for transfers between devices  306 us (40%)
  blocking collectives  149 us (20%)
  local copies, waits for them, and re-layouts  87.8 us (12%)
  other arithmetic  68.5 us (9%)
  matrix products  61 us (8%)
  starting transfers between devices  56.4 us (7%)
  between operations  17.6 us (2%)
    reduce_scatter x8, waiting for transfers between devices, body(): lax.psum_scatter(partial_rows(jnp.int32(0), shard_rows * lax.axis_size('t...  151 us
    all_gather x9, blocking collectives, body(): gathered = lax.all_gather(normed, 'tensor', axis=0, tiled=True)  65 us
    all_gather x9, blocking collectives, body(): gathered = lax.all_gather(current, 'tensor', axis=0, tiled=True)  63.2 us
    all_gather x1, waiting for transfers between devices, all_parts(): parts = lax.all_gather(block, name, axis=0, tiled=False)  58.6 us
    ppermute x16, waiting for transfers between devices, passed_along(): lax.ppermute(array, axis, [(i, (i + by) % peers) for i in range(peers)])  49.2 us
    while x2, local copies, waits for them, and re-layouts, body(): lax.fori_loop(0, pieces[0].shape[1] // group_size, one_group, (empty, emp...  47.2 us
    ppermute x16, starting transfers between devices, passed_along(): lax.ppermute(array, axis, [(i, (i + by) % peers) for i in range(peers)])  39.4 us
    add x2, other arithmetic, one_group(): updated.append(totals[factor_pick] + jnp.stack(partials, 1)[:, :, None, :])  37.3 us
  transfers between devices with their start and end apart: 31, of which 28 were waited for; matrix products, arithmetic and copies ran while one was open for 7% of the time, Pallas kernels for 0%

profile of v1, /device:TPU:0, one launch (start us, length us, event | category | flops | bytes accessed | tf_op | source)
XLA Modules:
  0.0 747.0 jit_solution(4871965243520608933)
XLA Ops:
  12.7 8.6 %all_gather.60 = bf16[64,4096]{1,0:T(8,128)(2,1)S(1)} all-gather(bf16[16,4096]{1,0:T(8,128)(2,1)S(1)} %fusion.157), channel_id=1, replica_groups=mesh['pipe'=4,'tensor'=4,'dp'=2] {'tensor'}, dimensions={0}, use_global_device_ids=true | all-gather | bytes 655360 | tf_op jit(solution)/shard_map/all_gather | solution.py:65
  21.4 5.6 conditional.16
  21.4 5.6 fusion.6
  30.4 4.5 all-to-all-done
  35.2 6.6 collective-permute-done
  42.1 7.0 all_gather.61
  49.1 5.1 conditional.17
  49.1 5.1 fusion.16
  54.2 7.0 all_to_all.104
  61.4 6.7 collective-permute-done.1
  68.4 7.0 all_gather.62
  75.4 7.0 all_to_all.105
  82.4 3.6 collective-permute-start.2
  89.5 7.0 all_gather.63
  96.5 7.1 all_to_all.106
  105.5 6.1 collective-permute-done.3
  111.9 7.0 all_gather.64
  118.8 5.8 conditional.20
  118.8 5.8 fusion.46
  128.0 4.5 all-to-all-done.4
  132.7 7.0 all-gather
  141.3 7.7 %all_gather.65 = bf16[64,4096]{1,0:T(8,128)(2,1)} all-gather(bf16[16,4096]{1,0:T(8,128)(2,1)S(1)} %fusion.145), channel_id=1, replica_groups=mesh['pipe'=4,'tensor'=4,'dp'=2] {'tensor'}, dimensions={0}, use_global_device_ids=true | all-gather | bytes 655360 | tf_op jit(solution)/shard_map/all_gather | solution.py:65
  149.0 5.8 conditional.21
  149.0 5.8 fusion.56
  158.2 4.5 all-to-all-done.5
  162.9 7.9 %collective-permute-done.5 = bf16[16,4096]{1,0:T(8,128)(2,1)S(1)} collective-permute-done((bf16[16,4096]{1,0:T(8,128)(2,1)S(1)}, bf16[16,4096]{1,0:T(8,128)(2,1)S(1)}, u32[]{:S(2)}, u32[]{:S(2)}) %collective-permute-start.5) | collective-permute-done | bytes 131104 | tf_op jit(solution)/shard_map/ppermute | solution.py:17
  171.0 7.0 all_gather.66
  182.0 4.5 all-to-all-done.6
  189.1 4.4 collective-permute-done.6
  193.7 7.0 all_gather.67
  204.7 4.5 all-to-all-done.7
  210.8 5.4 collective-permute-done.7
  219.2 6.3 collective-permute-start.8
  228.0 7.0 all_gather.71
  238.5 26.8 %reduce-scatter.11.cloned.1.call-done = bf16[16,4096]{1,0:T(8,128)(2,1)} async-done(((bf16[64,4096]{1,0:T(8,128)(2,1)}), bf16[16,4096]{1,0:T(8,128)(2,1)}) %reduce-scatter.11.cloned.1.call-update) | async-done | bytes 131088 | tf_op jit(solution)/shard_map/reduce_scatter | solution.py:113
  274.4 7.3 all_gather.72
  285.7 23.5 %reduce-scatter.13.cloned.1.call-done = bf16[16,4096]{1,0:T(8,128)(2,1)} async-done(((bf16[64,4096]{1,0:T(8,128)(2,1)}), bf16[16,4096]{1,0:T(8,128)(2,1)}) %reduce-scatter.13.cloned.1.call-update) | async-done | bytes 131088 | tf_op jit(solution)/shard_map/reduce_scatter | solution.py:113
  311.4 3.4 collective-permute-start.10
  317.3 6.9 all_gather.73
  324.3 6.9 conditional.27
  324.3 6.9 fusion.95
  334.4 16.6 %reduce-scatter.15.cloned.1.call-done = bf16[16,4096]{1,0:T(8,128)(2,1)} async-done(((bf16[64,4096]{1,0:T(8,128)(2,1)}), bf16[16,4096]{1,0:T(8,128)(2,1)}) %reduce-scatter.15.cloned.1.call-update) | async-done | bytes 131088 | tf_op jit(solution)/shard_map/reduce_scatter | solution.py:113
  359.1 6.9 all_gather.74
  366.0 6.9 conditional.28
  366.0 6.9 fusion.100
  376.1 20.3 %reduce-scatter.17.cloned.1.call-done = bf16[16,4096]{1,0:T(8,128)(2,1)} async-done(((bf16[64,4096]{1,0:T(8,128)(2,1)}), bf16[16,4096]{1,0:T(8,128)(2,1)}) %reduce-scatter.17.cloned.1.call-update) | async-done | bytes 131088 | tf_op jit(solution)/shard_map/reduce_scatter | solution.py:113
  404.5 6.9 all_gather.75
  415.5 26.3 %reduce-scatter.19.cloned.1.call-done = bf16[16,4096]{1,0:T(8,128)(2,1)} async-done(((bf16[64,4096]{1,0:T(8,128)(2,1)}), bf16[16,4096]{1,0:T(8,128)(2,1)}) %reduce-scatter.19.cloned.1.call-update) | async-done | bytes 131088 | tf_op jit(solution)/shard_map/reduce_scatter | solution.py:113
  443.9 3.4 collective-permute-start.13
  450.5 6.9 all_gather.76
  459.3 25.9 %reduce-scatter.21.cloned.1.call-done = bf16[16,4096]{1,0:T(8,128)(2,1)} async-done(((bf16[64,4096]{1,0:T(8,128)(2,1)}), bf16[16,4096]{1,0:T(8,128)(2,1)}) %reduce-scatter.21.cloned.1.call-update) | async-done | bytes 131088 | tf_op jit(solution)/shard_map/reduce_scatter | solution.py:113
  490.8 6.9 all_gather.68
  497.8 7.7 %all_gather.77 = bf16[64,4096]{1,0:T(8,128)(2,1)} all-gather(bf16[16,4096]{1,0:T(8,128)(2,1)S(1)} %collective-permute-done.14), channel_id=1, replica_groups=mesh['pipe'=4,'tensor'=4,'dp'=2] {'tensor'}, dimensions={0}, use_global_device_ids=true | all-gather | bytes 655360 | tf_op jit(solution)/shard_map/all_gather | solution.py:93
  519.3 11.0 %reduce-scatter.23.cloned.1.call-done = bf16[16,4096]{1,0:T(8,128)(2,1)} async-done(((bf16[64,4096]{1,0:T(8,128)(2,1)}), bf16[16,4096]{1,0:T(8,128)(2,1)}) %reduce-scatter.23.cloned.1.call-update) | async-done | bytes 131088 | tf_op jit(solution)/shard_map/reduce_scatter | solution.py:113
  538.4 6.5 all_gather.78
  546.4 25.0 %all-gather.4.cloned.1.call-done = bf16[2,256,4096]{2,1,0:T(8,128)(2,1)} async-done(((bf16[2,128,4096]{2,1,0:T(8,128)(2,1)}), bf16[2,256,4096]{2,1,0:T(8,128)(2,1)}) %all-gather.4.cloned.1.call-update) | async-done | bytes 4194320 | tf_op jit(solution)/shard_map/all_gather | solution.py:137
  571.5 58.6 %all-gather.6.cloned.1.call-done = bf16[2,2,128,4096]{3,2,0,1:T(8,128)(2,1)} async-done(((bf16[1,2,128,4096]{3,2,0,1:T(8,128)(2,1)}), bf16[2,2,128,4096]{3,2,0,1:T(8,128)(2,1)}) %all-gather.6.cloned.1.call-update) | async-done | bytes 4194320 | tf_op jit(solution)/shard_map/all_gather | solution.py:10
  630.1 62.1 %while.18 = (s32[]{:T(128)}, f32[512,2,1,4096]{3,0,1,2:T(8,128)}, f32[512,2,1,4096]{3,0,1,2:T(8,128)}, bf16[2,256,4096]{2,1,0:T(8,128)(2,1)}, s32[]{:T(128)}, /*...) while((s32[]{:T(128)}, f32[512,2,1,4096]{3,0,1,2:T(8,128)}, ...), condition=%wide.region_66.67_spmd.clone, body=%wide.region_65.66_spmd.clone.sunk | while | flops 2197815296 | bytes 105390264 | solution.py:159
  632.7 4.6 multiply_convert_fusion.10
  642.5 14.2 %convert_add_fusion.12 = (f32[512,2,1,4096]{3,0,1,2:T(8,128)}, f32[512,2,1,4096]{3,0,1,2:T(8,128)}) fusion(f32[512,2,1,4096]{3,0,1,2:T(8,128)} %get-tuple-element.770, bf16[512,1,4096]{2,0,1:T(8,128)(2,1)S(1)} %bitcast.338, bf16[512,1,4096]{2,0,1:T(8,128)(2,1)S(1)} %bitcast.336, pred[]{:T(512)S(6)} %compare.57, bf16[512,1,4096]{2,0,1:T(8,128)(2,1)} %bitcast.339, ...), kind=kLoop, calls=%fused_computation.88.clone.1 | loop fusion | flops 33554432 | bytes 83886080 | tf_op jit(solution)/shard_map/while/body/eval_jaxpr/add | solution.py:156
  659.2 4.6 multiply_convert_fusion.10
  669.1 23.1 %convert_add_fusion.12 = (f32[512,2,1,4096]{3,0,1,2:T(8,128)}, f32[512,2,1,4096]{3,0,1,2:T(8,128)}) fusion(f32[512,2,1,4096]{3,0,1,2:T(8,128)} %get-tuple-element.770, bf16[512,1,4096]{2,0,1:T(8,128)(2,1)S(1)} %bitcast.338, bf16[512,1,4096]{2,0,1:T(8,128)(2,1)S(1)} %bitcast.336, pred[]{:T(512)S(6)} %compare.57, bf16[512,1,4096]{2,0,1:T(8,128)(2,1)} %bitcast.339, ...), kind=kLoop, calls=%fused_computation.88.clone.1 | loop fusion | flops 33554432 | bytes 83886080 | tf_op jit(solution)/shard_map/while/body/eval_jaxpr/add | solution.py:156
  692.2 28.6 %copy.39 = bf16[512,2,1,4096]{3,1,2,0:T(2,128)(2,1)} copy(f32[512,2,1,4096]{3,0,1,2:T(8,128)} %get-tuple-element.635) | data formatting | bytes 25165824 | tf_op jit(solution)/shard_map/while | solution.py:159
  720.7 18.6 %copy.40 = bf16[512,2,1,4096]{3,1,2,0:T(2,128)(2,1)} copy(f32[512,2,1,4096]{3,0,1,2:T(8,128)S(1)} %copy-done) | data formatting | bytes 25165824 | tf_op jit(solution)/shard_map/while | solution.py:159
  (205 shorter events, 144.5 us)
Async XLA Ops:
  8.0 27.0 %copy-start.3 = (bf16[2,16,4096]{2,1,0:T(8,128)(2,1)S(1)}, bf16[2,16,4096]{2,1,0:T(8,128)(2,1)}, u32[]{:S(2)}) copy-start(bf16[2,16,4096]{2,1,0:T(8,128)(2,1)} %param.38) | copy-start | bytes 786436
  27.0 7.9 %all-to-all-start = ((bf16[4,16,1024]{2,1,0:T(8,128)(2,1)}), bf16[4,16,1024]{2,1,0:T(8,128)(2,1)S(1)}, u32[]{:S(2)}, u32[]{:S(2)}) async-start(bf16[4,16,1024]{2,1,0:T(8,128)(2,1)} %bitcast.29), calls=%async_computation | async-start | bytes 262144 | tf_op jit(solution)/shard_map/all_to_all | solution.py:77
  35.0 6.8 collective-permute-start
  61.3 6.8 collective-permute-start.1
  82.4 6.8 collective-permute-start.2
  96.5 31.5 %copy-start.4 = (bf16[2,16,4096]{2,1,0:T(8,128)(2,1)S(1)}, bf16[2,16,4096]{2,1,0:T(8,128)(2,1)}, u32[]{:S(2)}) copy-start(bf16[2,16,4096]{2,1,0:T(8,128)(2,1)} %param.41) | copy-start | bytes 786436
  103.7 7.9 %collective-permute-start.3 = (bf16[16,4096]{1,0:T(8,128)(2,1)S(1)}, bf16[16,4096]{1,0:T(8,128)(2,1)S(1)}, u32[]{:S(2)}, u32[]{:S(2)}) collective-permute-start(bf16[16,4096]{1,0:T(8,128)(2,1)S(1)} %fusion.138), channel_id=1, source_target_pairs={{0,8},{8,16},{16,24},{24,0},{1,9},{9,17},{17,25},{25,1},{2,10},{10... | collective-permute-start | bytes 393224 | tf_op jit(solution)/shard_map/ppermute | solution.py:17
  124.6 7.9 %all-to-all-start.4 = ((bf16[4,16,1024]{2,1,0:T(8,128)(2,1)}), bf16[4,16,1024]{2,1,0:T(8,128)(2,1)S(1)}, u32[]{:S(2)}, u32[]{:S(2)}) async-start(bf16[4,16,1024]{2,1,0:T(8,128)(2,1)} %bitcast.45), calls=%async_computation.4 | async-start | bytes 262144 | tf_op jit(solution)/shard_map/all_to_all | solution.py:77
  127.9 88.2 %reduce-scatter.9.cloned.1.call-start = ((), (), s32[]{:S(2)}) async-start(), calls=%async_computation.17 | async-start | bytes 655360 | tf_op jit(solution)/shard_map/reduce_scatter | solution.py:113
  132.6 8.4 %collective-permute-start.4 = (bf16[16,4096]{1,0:T(8,128)(2,1)S(1)}, bf16[16,4096]{1,0:T(8,128)(2,1)S(1)}, u32[]{:S(2)}, u32[]{:S(2)}) collective-permute-start(bf16[16,4096]{1,0:T(8,128)(2,1)S(1)} %fusion.142), channel_id=1, source_target_pairs={{0,8},{8,16},{16,24},{24,0},{1,9},{9,17},{17,25},{25,1},{2,10},{10... | collective-permute-start | bytes 393224 | tf_op jit(solution)/shard_map/ppermute | solution.py:17
  139.8 0.8 copy-start.1
  154.8 7.9 %all-to-all-start.5 = ((bf16[4,16,1024]{2,1,0:T(8,128)(2,1)}), bf16[4,16,1024]{2,1,0:T(8,128)(2,1)S(1)}, u32[]{:S(2)}, u32[]{:S(2)}) async-start(bf16[4,16,1024]{2,1,0:T(8,128)(2,1)} %bitcast.49), calls=%async_computation.5 | async-start | bytes 262144 | tf_op jit(solution)/shard_map/all_to_all | solution.py:77
  162.8 7.9 %collective-permute-start.5 = (bf16[16,4096]{1,0:T(8,128)(2,1)S(1)}, bf16[16,4096]{1,0:T(8,128)(2,1)S(1)}, u32[]{:S(2)}, u32[]{:S(2)}) collective-permute-start(bf16[16,4096]{1,0:T(8,128)(2,1)S(1)} %fusion.146), channel_id=1, source_target_pairs={{0,8},{8,16},{16,24},{24,0},{1,9},{9,17},{17,25},{25,1},{2,10},{10... | collective-permute-start | bytes 393224 | tf_op jit(solution)/shard_map/ppermute | solution.py:17
  178.6 7.9 %all-to-all-start.6 = ((bf16[4,16,1024]{2,1,0:T(8,128)(2,1)}), bf16[4,16,1024]{2,1,0:T(8,128)(2,1)S(1)}, u32[]{:S(2)}, u32[]{:S(2)}) async-start(bf16[4,16,1024]{2,1,0:T(8,128)(2,1)} %bitcast.53), calls=%async_computation.6 | async-start | bytes 262144 | tf_op jit(solution)/shard_map/all_to_all | solution.py:77
  186.6 6.8 collective-permute-start.6
  201.3 7.9 %all-to-all-start.7 = ((bf16[4,16,1024]{2,1,0:T(8,128)(2,1)}), bf16[4,16,1024]{2,1,0:T(8,128)(2,1)S(1)}, u32[]{:S(2)}, u32[]{:S(2)}) async-start(bf16[4,16,1024]{2,1,0:T(8,128)(2,1)} %bitcast.57), calls=%async_computation.7 | async-start | bytes 262144 | tf_op jit(solution)/shard_map/all_to_all | solution.py:77
  204.7 60.7 %reduce-scatter.11.cloned.1.call-start = ((), (), s32[]{:S(2)}) async-start(), calls=%async_computation.18 | async-start | bytes 655360 | tf_op jit(solution)/shard_map/reduce_scatter | solution.py:113
  209.3 6.8 collective-permute-start.7
  219.2 8.8 %collective-permute-start.8 = (bf16[16,4096]{1,0:T(8,128)(2,1)S(1)}, bf16[16,4096]{1,0:T(8,128)(2,1)S(1)}, u32[]{:S(2)}, u32[]{:S(2)}) collective-permute-start(bf16[16,4096]{1,0:T(8,128)(2,1)S(1)} %fusion.162), channel_id=1, source_target_pairs={{0,24},{8,0},{16,8},{24,16},{1,25},{9,1},{17,9},{25,17},{2,26},{10... | collective-permute-start | bytes 393224 | tf_op jit(solution)/shard_map/ppermute | solution.py:17
  235.0 0.8 copy-start.2
  235.9 73.4 %reduce-scatter.13.cloned.1.call-start = ((), (), s32[]{:S(2)}) async-start(), calls=%async_computation.19 | async-start | bytes 655360 | tf_op jit(solution)/shard_map/reduce_scatter | solution.py:113
  268.1 6.3 collective-permute-start.9
  282.6 68.5 %reduce-scatter.15.cloned.1.call-start = ((), (), s32[]{:S(2)}) async-start(), calls=%async_computation.20 | async-start | bytes 655360 | tf_op jit(solution)/shard_map/reduce_scatter | solution.py:113
  311.4 6.0 collective-permute-start.10
  331.2 65.1 %reduce-scatter.17.cloned.1.call-start = ((), (), s32[]{:S(2)}) async-start(), calls=%async_computation.21 | async-start | bytes 655360 | tf_op jit(solution)/shard_map/reduce_scatter | solution.py:113
  353.1 6.0 collective-permute-start.11
  373.0 68.7 %reduce-scatter.19.cloned.1.call-start = ((), (), s32[]{:S(2)}) async-start(), calls=%async_computation.22 | async-start | bytes 655360 | tf_op jit(solution)/shard_map/reduce_scatter | solution.py:113
  398.5 6.0 collective-permute-start.12
  412.3 73.0 %reduce-scatter.21.cloned.1.call-start = ((), (), s32[]{:S(2)}) async-start(), calls=%async_computation.23 | async-start | bytes 655360 | tf_op jit(solution)/shard_map/reduce_scatter | solution.py:113
  443.9 6.0 collective-permute-start.13
  449.9 0.6 copy-start.5
  458.5 71.8 %reduce-scatter.23.cloned.1.call-start = ((), (), s32[]{:S(2)}) async-start(), calls=%async_computation.24 | async-start | bytes 655360 | tf_op jit(solution)/shard_map/reduce_scatter | solution.py:113
  487.5 10.3 %collective-permute-start.14 = (bf16[16,4096]{1,0:T(8,128)(2,1)S(1)}, bf16[16,4096]{1,0:T(8,128)(2,1)S(1)}, u32[]{:S(2)}, u32[]{:S(2)}) collective-permute-start(bf16[16,4096]{1,0:T(8,128)(2,1)S(1)} %fusion.192), channel_id=1, source_target_pairs={{0,24},{8,0},{16,8},{24,16},{1,25},{9,1},{17,9},{25,17},{2,26},{10... | collective-permute-start | bytes 393224 | tf_op jit(solution)/shard_map/ppermute | solution.py:17
  506.4 65.1 %all-gather.4.cloned.1.call-start = ((), (), s32[]{:S(2)}) async-start(), calls=%async_computation.16 | async-start | bytes 6291456 | tf_op jit(solution)/shard_map/all_gather | solution.py:137
  512.7 117.4 %all-gather.6.cloned.1.call-start = ((), (), s32[]{:S(2)}) async-start(), calls=%async_computation.25 | async-start | bytes 6291456 | tf_op jit(solution)/shard_map/all_gather | solution.py:10
  532.4 6.0 collective-permute-start.15
  692.2 28.6 %copy-start = (f32[512,2,1,4096]{3,0,1,2:T(8,128)S(1)}, f32[512,2,1,4096]{3,0,1,2:T(8,128)}, u32[]{:S(2)}) copy-start(f32[512,2,1,4096]{3,0,1,2:T(8,128)} %get-tuple-element.634) | copy-start | bytes 50331652
Sparse Core Ops, SparseCore 0:
  140.8 28.8 reduce-scatter.8
  236.0 29.3 reduce-scatter.10
  282.7 26.5 reduce-scatter.12
  331.4 19.5 reduce-scatter.14
  373.1 23.2 reduce-scatter.16
  412.4 29.3 reduce-scatter.18
  458.6 26.6 reduce-scatter.20
  506.5 23.7 reduce-scatter.22
Sparse Core Ops, SparseCore 1:
  512.7 58.7 all-gather.3
  573.5 56.6 all-gather.5
